TPU v7x, 32 devices: a whole 2x2x4 slice. The times are simulated.
32 devices in a mesh: ctx: 8 (over y, x, core), chan: 4 (over z).
Axes of the slice: x: 2, y: 2, z: 4, core: 2. Of those that a mesh axis runs over, the one named last changes fastest.
Arguments:
- queries: bfloat16 [1024, 4096], P('ctx', 'chan'), may hold values from -8 to 8
- key_rows: bfloat16 [1024, 4096], P('ctx', 'chan'), may hold values from -8 to 8
- value_rows: bfloat16 [1024, 4096], P('ctx', 'chan'), may hold values from -16 to 16
- gate_in: bfloat16 [1024, 4096], P('ctx', 'chan'), may hold values from -6 to 6
- gate_out: bfloat16 [1024, 4096], P('ctx', 'chan'), may hold values from -6 to 6
- kernel_taps: float32 [512, 7], P('chan'), may hold values from -2 to 2
- norm_gain: float32 [4096], P('chan'), may hold values from 0.1 to 1.9
- cotangent: bfloat16 [1024, 4096], P('ctx', 'chan'), may hold values from -6 to 6
Outputs:
- mixed: bfloat16 [1024, 4096], P('ctx', 'chan')
- grad_queries: bfloat16 [1024, 4096], P('ctx', 'chan')
- grad_keys: bfloat16 [1024, 4096], P('ctx', 'chan')
- grad_values: bfloat16 [1024, 4096], P('ctx', 'chan')
- grad_gate_in: bfloat16 [1024, 4096], P('ctx', 'chan')
- grad_gate_out: bfloat16 [1024, 4096], P('ctx', 'chan')
- grad_filter: float32 [512, 7], P('chan')
- grad_gain: float32 [4096], P('chan')
All inputs are finite; a program needn't handle non-finite values.
Results may differ from a plain program's by a relative error of at most 0.015.
Values may be sent and summed in bfloat16 or wider, within the bound.
No kernel may reach another device: no remote copies, remote signals or barrier semaphores. Data moves between devices by JAX's collectives and lax.ppermute only.
A program may use at most 128 MiB of HBM per device.

v0:
```python
import jax
import jax.numpy as jnp
from jax import lax
from jax.sharding import PartitionSpec as P

HEAD = 128
FILT = 7
WIDTH = 4096
EPS = 1e-06
NEG = -1e30


def from_behind(shard, axis, by):
    length = lax.axis_size(axis)
    pairs = [(i, i + by) for i in range(length) if 0 <= i + by < length]
    return lax.ppermute(shard, axis, pairs)


def score_block(query_heads, key_block, query_pos, key_pos):
    scores = jnp.einsum(
        "rhe,khe->hrk", query_heads, key_block, preferred_element_type=jnp.float32
    ) * HEAD ** (-0.5)
    allowed = query_pos[:, None] >= key_pos[None, :]
    return jnp.where(allowed[None], scores, NEG)


def row_totals(query_heads, query_pos, block_count, keys_heads, block_rows):
    row_count = query_heads.shape[0]
    head_count = query_heads.shape[1]

    def advance(block_index, running):
        row_max, row_sum = running
        first_key = block_index * block_rows
        key_block = lax.dynamic_slice_in_dim(keys_heads, first_key, block_rows, 0)
        key_pos = first_key + jnp.arange(block_rows, dtype=jnp.int32)
        scores = score_block(query_heads, key_block, query_pos, key_pos)
        new_max = jnp.maximum(row_max, jnp.max(scores, axis=2))
        row_sum = row_sum * jnp.exp(row_max - new_max) + jnp.sum(
            jnp.exp(scores - new_max[:, :, None]), axis=2
        )
        return (new_max, row_sum)

    initial = (
        jnp.full((head_count, row_count), NEG, jnp.float32),
        jnp.zeros((head_count, row_count), jnp.float32),
    )
    row_max, row_sum = lax.fori_loop(0, block_count, advance, initial)
    return row_max + jnp.log(row_sum)


def row_outputs(query_heads, query_pos, block_count, keys_heads, values_heads, lse, block_rows):
    row_count = query_heads.shape[0]
    head_count = query_heads.shape[1]

    def advance(block_index, summed):
        first_key = block_index * block_rows
        key_block = lax.dynamic_slice_in_dim(keys_heads, first_key, block_rows, 0)
        value_block = lax.dynamic_slice_in_dim(values_heads, first_key, block_rows, 0)
        key_pos = first_key + jnp.arange(block_rows, dtype=jnp.int32)
        scores = score_block(query_heads, key_block, query_pos, key_pos)
        weights_low = jnp.exp(scores - lse[:, :, None]).astype(jnp.bfloat16)
        return summed + jnp.einsum(
            "hrk,khe->rhe", weights_low, value_block, preferred_element_type=jnp.float32
        )

    summed = lax.fori_loop(
        0, block_count, advance, jnp.zeros((row_count, head_count, HEAD), jnp.float32)
    )
    return summed.reshape(row_count, head_count * HEAD).astype(jnp.bfloat16)


def query_grads(
    query_heads, d_heads, query_pos, block_count, keys_heads, values_heads, lse, delta, block_rows
):
    row_count = query_heads.shape[0]
    head_count = query_heads.shape[1]

    def advance(block_index, summed):
        first_key = block_index * block_rows
        key_block = lax.dynamic_slice_in_dim(keys_heads, first_key, block_rows, 0)
        value_block = lax.dynamic_slice_in_dim(values_heads, first_key, block_rows, 0)
        key_pos = first_key + jnp.arange(block_rows, dtype=jnp.int32)
        scores = score_block(query_heads, key_block, query_pos, key_pos)
        weights = jnp.exp(scores - lse[:, :, None])
        d_probs = jnp.einsum(
            "rhe,khe->hrk", d_heads, value_block, preferred_element_type=jnp.float32
        )
        d_scores = (weights * (d_probs - delta[:, :, None])).astype(jnp.bfloat16)
        return summed + jnp.einsum(
            "hrk,khe->rhe", d_scores, key_block, preferred_element_type=jnp.float32
        )

    summed = lax.fori_loop(
        0, block_count, advance, jnp.zeros((row_count, head_count, HEAD), jnp.float32)
    )
    return (summed * HEAD ** (-0.5)).reshape(row_count, head_count * HEAD).astype(jnp.bfloat16)


def shards(queries, key_rows, value_rows, gate_in, gate_out, kernel_taps, norm_gain, cotangent):
    row_count = queries.shape[0]
    channels = queries.shape[1]
    head_count = channels // HEAD
    group_count = kernel_taps.shape[0]
    devices = lax.axis_size("ctx")
    position = lax.axis_index("ctx")
    own_first = position * row_count
    total_rows = row_count * devices
    block_rows = min(512, total_rows)
    local_pos = jnp.arange(row_count, dtype=jnp.int32)
    keys_all, values_all = (
        lax.all_gather(key_rows, "ctx", axis=0, tiled=True),
        lax.all_gather(value_rows, "ctx", axis=0, tiled=True),
    )
    keys_heads = keys_all.reshape(total_rows, head_count, HEAD)
    query_sets = (queries, own_first + local_pos)
    query_block, query_pos = query_sets
    block_count = query_pos[-1] // block_rows + 1
    lse_sets = row_totals(
        query_block.reshape(-1, head_count, HEAD), query_pos, block_count, keys_heads, block_rows
    )
    values_heads = values_all.reshape(total_rows, head_count, HEAD)
    query_block, query_pos = query_sets
    outputs = row_outputs(
        query_block.reshape(-1, head_count, HEAD),
        query_pos,
        block_count,
        keys_heads,
        values_heads,
        lse_sets,
        block_rows,
    )
    lse_rows = lse_sets.T
    attn_wide = outputs.astype(jnp.float32)
    square_sum = lax.psum(jnp.sum(attn_wide * attn_wide, axis=1), "chan")
    inverse_rms = 1.0 / jnp.sqrt(square_sum / WIDTH + EPS)
    normed = attn_wide * inverse_rms[:, None] * norm_gain[None, :]
    gate_wide = gate_in.astype(jnp.float32)
    mixed_in = gate_wide * normed
    taps = jnp.broadcast_to(
        kernel_taps[:, None, :], (group_count, channels // group_count, FILT)
    ).reshape(channels, FILT)
    rim_before = from_behind(mixed_in[row_count - (FILT - 1) :], "ctx", 1)
    extended = jnp.concatenate([rim_before, mixed_in], axis=0)
    conv_out = jnp.zeros((row_count, channels), jnp.float32)
    for lag in range(FILT):
        conv_out = (
            conv_out + taps[:, lag][None, :] * extended[FILT - 1 - lag : FILT - 1 - lag + row_count]
        )
    out_gate = gate_out.astype(jnp.float32)
    mixed = (out_gate * conv_out).astype(jnp.bfloat16)
    upstream = cotangent.astype(jnp.float32)
    grad_gate_out = (upstream * conv_out).astype(jnp.bfloat16)
    d_conv = upstream * out_gate
    tap_columns = []
    for lag in range(FILT):
        per_channel = jnp.sum(
            d_conv * extended[FILT - 1 - lag : FILT - 1 - lag + row_count], axis=0
        )
        tap_columns.append(per_channel.reshape(group_count, -1).sum(axis=1))
    tap_terms = jnp.stack(tap_columns, axis=1)
    rim_after = from_behind(d_conv[: FILT - 1], "ctx", -1)
    extended_grad = jnp.concatenate([d_conv, rim_after], axis=0)
    d_mixed = jnp.zeros((row_count, channels), jnp.float32)
    for lag in range(FILT):
        d_mixed = d_mixed + taps[:, lag][None, :] * extended_grad[lag : lag + row_count]
    grad_gate_in = (d_mixed * normed).astype(jnp.bfloat16)
    d_normed = d_mixed * gate_wide
    gain_terms = jnp.sum(d_normed * attn_wide * inverse_rms[:, None], axis=0)
    grad_filter, grad_gain = lax.psum((tap_terms, gain_terms), "ctx")
    scaled = d_normed * norm_gain[None, :]
    row_dot = lax.psum(jnp.sum(scaled * attn_wide, axis=1), "chan")
    d_attn = (
        inverse_rms[:, None] * scaled - attn_wide * (inverse_rms**3 * row_dot / WIDTH)[:, None]
    ).astype(jnp.bfloat16)
    d_heads = d_attn.reshape(row_count, head_count, HEAD)
    delta_rows = jnp.sum(
        d_heads.astype(jnp.float32) * attn_wide.reshape(row_count, head_count, HEAD), axis=2
    )
    own_count = (own_first + row_count - 1) // block_rows + 1
    grad_queries = query_grads(
        queries.reshape(row_count, head_count, HEAD),
        d_heads,
        own_first + local_pos,
        own_count,
        keys_heads,
        values_heads,
        lse_rows.T,
        delta_rows.T,
        block_rows,
    )
    lse_all, delta_all = (
        lax.all_gather(lse_rows, "ctx", axis=0, tiled=True),
        lax.all_gather(delta_rows, "ctx", axis=0, tiled=True),
    )
    own_keys = key_rows.reshape(row_count, head_count, HEAD)
    own_values = value_rows.reshape(row_count, head_count, HEAD)
    key_pos = own_first + local_pos
    empty_grad = jnp.zeros((row_count, head_count, HEAD), jnp.float32)
    query_piece = lax.all_gather(queries, "ctx", axis=0, tiled=True)
    d_piece = lax.all_gather(d_attn, "ctx", axis=0, tiled=True)
    piece_rows = query_piece.shape[0]

    def contribute(totals):
        query_heads = query_piece.reshape(piece_rows, head_count, HEAD)
        piece_heads = d_piece.reshape(piece_rows, head_count, HEAD)
        query_pos = jnp.arange(piece_rows, dtype=jnp.int32)
        lse_piece = lse_all.T
        delta_piece = delta_all.T
        scores = score_block(query_heads, own_keys, query_pos, key_pos)
        weights = jnp.exp(scores - lse_piece[:, :, None])
        d_probs = jnp.einsum(
            "rhe,khe->hrk", piece_heads, own_values, preferred_element_type=jnp.float32
        )
        d_scores = (weights * (d_probs - delta_piece[:, :, None])).astype(jnp.bfloat16)
        key_grad = jnp.einsum(
            "hrk,rhe->khe", d_scores, query_heads, preferred_element_type=jnp.float32
        )
        value_grad = jnp.einsum(
            "hrk,rhe->khe",
            weights.astype(jnp.bfloat16),
            piece_heads,
            preferred_element_type=jnp.float32,
        )
        return (key_grad, value_grad)

    def unchanged(totals):
        return totals

    key_grad, value_grad = lax.cond(
        jnp.int32(0) + piece_rows > own_first, contribute, unchanged, (empty_grad, empty_grad)
    )
    grad_keys = (key_grad * HEAD ** (-0.5)).reshape(row_count, channels).astype(jnp.bfloat16)
    grad_values = value_grad.reshape(row_count, channels).astype(jnp.bfloat16)
    return (
        mixed,
        grad_queries,
        grad_keys,
        grad_values,
        grad_gate_in,
        grad_gate_out,
        grad_filter,
        grad_gain,
    )


def solution(mesh):
    placed = (
        P("ctx", "chan"),
        P("ctx", "chan"),
        P("ctx", "chan"),
        P("ctx", "chan"),
        P("ctx", "chan"),
        P("chan", None),
        P("chan"),
        P("ctx", "chan"),
    )
    return jax.shard_map(
        shards,
        mesh=mesh,
        in_specs=placed,
        out_specs=(
            P("ctx", "chan"),
            P("ctx", "chan"),
            P("ctx", "chan"),
            P("ctx", "chan"),
            P("ctx", "chan"),
            P("ctx", "chan"),
            P("chan", None),
            P("chan"),
        ),
        check_vma=False,
    )
```

profile of v0, /device:TPU:0, one launch (start us, length us, event | category | flops | bytes accessed | tf_op | source)
XLA Modules:
  0.0 189.7 jit_solution(9424736942254590684)
XLA Ops:
  7.2 1.8 copy.75
  9.1 1.8 copy.74
  11.0 1.1 convert_multiply_fusion.1
  12.1 0.8 copy-done.3
  12.9 1.3 collective-permute-start.1
  14.3 0.6 slice.80
  16.8 0.2 copy.76
  17.7 0.2 copy.80
  17.9 0.2 broadcast_in_dim.76
  18.1 0.2 reshape.211
  18.3 23.0 %all-gather.7.cloned.1.call-done = bf16[1024,1024]{0,1:T(8,128)(2,1)} async-done(((bf16[128,1024]{0,1:T(8,128)(2,1)}), bf16[1024,1024]{0,1:T(8,128)(2,1)}) %all-gather.7.cloned.1.call-update) | async-done | bytes 2097168 | tf_op jit(solution)/shard_map/all_gather | solution.py:111
  41.3 3.0 %copy.79 = bf16[1024,8,128]{2,0,1:T(8,128)(2,1)S(1)} copy(bf16[1024,8,128]{0,2,1:T(8,128)(2,1)} %bitcast.151) | data formatting | bytes 4194304
  44.4 1.2 while.35
  44.4 0.1 broadcast_compare_fusion.6
  44.6 0.5 fusion.130
  45.1 0.4 exponential_reduce_fusion.2
  45.6 26.3 %all-gather.5.cloned.1.call-done = bf16[1024,1024]{0,1:T(8,128)(2,1)} async-done(((bf16[128,1024]{0,1:T(8,128)(2,1)}), bf16[1024,1024]{0,1:T(8,128)(2,1)}) %all-gather.5.cloned.1.call-update) | async-done | bytes 2097168 | tf_op jit(solution)/shard_map/all_gather | solution.py:112
  71.9 2.4 %while.36 = (s32[]{:T(128)}, f32[128,8,128]{0,2,1:T(8,128)S(1)}, s32[]{:T(128)}, bf16[1024,8,128]{0,2,1:T(8,128)(2,1)}, bf16[1024,8,128]{2,0,1:T(8,128)(2,1)S(1)...) while((s32[]{:T(128)}, f32[128,8,128]{0,2,1:T(8,128)S(1)}, ...), condition=%wide.region_5.6_spmd.clone, body=%wide.region_4.5_spmd.clone.sunk | while | flops 270729856 | bytes 3549363 | solution.py:66
  72.0 0.1 broadcast_compare_fusion.7
  72.1 2.2 %fusion.134 = f32[128,8,128]{0,2,1:T(8,128)S(1)} fusion(f32[128,8,128]{0,2,1:T(8,128)S(1)} %get-tuple-element.657, bf16[128,8,128]{2,0,1:T(8,128)(2,1)S(1)} %get-tuple-element.673, f32[8,128]{1,0:T(8,128)S(1)} %get-tuple-element.674, bf16[1024,8,128]{2,0,1:T(8,128)(2,1)S(1)} %get-tuple-element.672, s32[]{:T(128)S(6)} %select_n.93, ...), kind=kOutput, calls=%fused_computation.44.clone.1 | convolution fusion | flops 270663680 | bytes 3478528 | tf_op jit(solution)/shard_map/while/body/hrk,khe->rhe/dot_general | solution.py:62
  74.4 1.0 multiply_reduce_fusion.10
  75.3 11.7 %psum.28 = f32[128]{0:T(128)S(1)} all-reduce(f32[128]{0:T(128)S(1)} %get-tuple-element.441), channel_id=1, replica_groups=mesh['ctx'=8,'chan'=4] {'chan'}, use_global_device_ids=true, to_apply=%region_7.8 | all-reduce | flops 128 | bytes 1024 | tf_op jit(solution)/shard_map/psum | solution.py:134
  87.0 1.2 copy.97
  88.3 4.0 %multiply_convert_fusion.1 = (bf16[128,1024]{1,0:T(8,128)(2,1)}, f32[128,1024]{1,0:T(8,128)S(1)}) fusion(f32[128,1024]{1,0:T(8,128)S(1)} %copy.97, f32[1024]{0:T(1024)S(1)} %copy-done.10, f32[128]{0:T(128)S(1)} %add_rsqrt_fusion, f32[6,1024]{1,0:T(8,128)S(1)} %collective-permute-done.1, f32[128,1024]{1,0:T(8,128)} %copy-done.3, f32[1024]{0:T(1024)S(1)} %bitcast.162, ...), kind=kLoop, calls=%fused_computation.133 | loop fusion | flops 3014656 | bytes 1892864 | tf_op jit(solution)/shard_map/convert_element_type | solution.py:166
  92.3 0.8 copy-done.1
  93.1 0.2 multiply_reduce_fusion
  93.3 8.4 %psum.29 = f32[128]{0:T(128)S(1)} all-reduce(f32[128]{0:T(128)S(1)} %get-tuple-element.373), channel_id=1, replica_groups=mesh['ctx'=8,'chan'=4] {'chan'}, use_global_device_ids=true, to_apply=%region_9.10 | all-reduce | flops 128 | bytes 1024 | tf_op jit(solution)/shard_map/psum | solution.py:171
  101.7 2.0 %subtract_convert_fusion = (bf16[128,1024]{1,0:T(8,128)(2,1)}, f32[128,1024]{1,0:T(8,128)S(1)}) fusion(f32[128,1024]{1,0:T(8,128)S(1)} %copy.97, f32[128]{0:T(128)S(1)} %fusion.102, f32[1024]{0:T(1024)S(1)} %copy-done.10, f32[128]{0:T(128)S(1)} %add_rsqrt_fusion, f32[128,1024]{1,0:T(8,128)} %copy-done.1, bf16[128,1024]{1,0:T(8,128)(2,1)} %param.19), kind=kLoop, calls=%fused_computation.137 | loop fusion | flops 1310720 | bytes 2102272 | tf_op jit(solution)/shard_map/convert_element_type | solution.py:174
  103.8 0.6 slice.103
  104.4 1.3 collective-permute-start
  105.7 1.0 copy.109
  106.7 0.2 copy.82
  106.9 1.1 multiply_reduce_fusion.8
  108.0 1.0 copy_bitcast_fusion
  109.0 0.9 broadcast.128
  109.9 5.9 %while.37 = (s32[]{:T(128)}, f32[128,8,128]{0,2,1:T(8,128)}, s32[]{:T(128)}, bf16[1024,8,128]{2,0,1:T(8,128)(2,1)S(1)}, bf16[128,8,128]{2,0,1:T(8,128)(2,1)S(1)}...) while((s32[]{:T(128)}, f32[128,8,128]{0,2,1:T(8,128)}, ...), condition=%wide.region_12.13_spmd.clone, body=%wide.region_11.12_spmd.clone.sunk | while | flops 405996160 | bytes 9058503 | solution.py:93
  109.9 1.7 fusion.140
  111.7 0.1 broadcast_compare_fusion.8
  111.8 4.1 %fusion.141 = f32[128,8,128]{0,2,1:T(8,128)} fusion(f32[128,8,128]{0,2,1:T(8,128)} %get-tuple-element.695, f32[8,512,128]{2,1,0:T(8,128)} %fusion.140, bf16[128,8,128]{2,0,1:T(8,128)(2,1)S(1)} %get-tuple-element.715, f32[8,128]{1,0:T(8,128)S(1)} %get-tuple-element.716, bf16[1024,8,128]{0,2,1:T(8,128)(2,1)} %get-tuple-element.714, s32[]{:T(128)S(6)} %select_n.95, ...), kind=kOutput, calls=%fused_computation.64.clone.1 | convolution fusion | flops 271712256 | bytes 5579776 | tf_op jit(solution)/shard_map/while/body/hrk,khe->rhe/dot_general | solution.py:89
  115.9 1.1 multiply_convert_fusion.3
  117.0 0.9 copy.98
  117.9 17.9 %all_gather.23 = f32[1024,8]{0,1:T(8,128)S(1)} all-gather(f32[128,8]{0,1:T(8,128)S(1)} %bitcast.178), channel_id=1, replica_groups=mesh['ctx'=8,'chan'=4] {'ctx'}, dimensions={0}, use_global_device_ids=true | all-gather | bytes 36864 | tf_op jit(solution)/shard_map/all_gather | solution.py:193
  135.8 8.5 %all_gather.21 = f32[1024,8]{0,1:T(8,128)S(1)} all-gather(f32[128,8]{0,1:T(8,128)S(1)} %bitcast.179), channel_id=1, replica_groups=mesh['ctx'=8,'chan'=4] {'ctx'}, dimensions={0}, use_global_device_ids=true | all-gather | bytes 36864 | tf_op jit(solution)/shard_map/all_gather | solution.py:192
  144.3 1.2 fusion.78
  145.5 1.2 multiply_reduce_fusion.1
  146.9 0.1 reshape.217
  147.0 0.1 reshape.219
  147.4 0.1 reduce_sum.175
  147.5 0.1 reduce_sum.177
  147.6 0.1 reduce_sum.179
  147.7 0.1 reduce_sum.181
  147.8 0.1 reduce_sum.183
  148.0 0.1 reduce_sum.185
  148.1 0.1 reduce_sum.187
  148.2 14.2 %all-reduce = (f32[128,7]{0,1:T(8,128)}, f32[1024]{0:T(1024)}) all-reduce(f32[128,7]{0,1:T(8,128)S(1)} %stack.31, f32[1024]{0:T(1024)S(1)} %get-tuple-element.372), channel_id=1, replica_groups=mesh['ctx'=8,'chan'=4] {'ctx'}, use_global_device_ids=true, to_apply=%region_29.30 | all-reduce | flops 1920 | bytes 15360 | tf_op jit(solution)/shard_map/psum | solution.py:169
  162.5 19.8 %conditional.1 = (f32[128,8,128]{0,2,1:T(8,128)S(1)}, bf16[128,1024]{1,0:T(8,128)(2,1)}) conditional(s32[]{:T(128)} %convert_element_type.91, () %tuple.33, (s32[128]{0:T(128)S(1)}, bf16[1024,1024]{1,0:T(8,128)(2,1)}, bf16[128,1024]{1,0:T(8,128)(2,1)S(1)}, f32[1024,8]{0,1:T(8,128)S(1)}, bf16[1024,1024]{1,0:T(8,128)(2,1)}, ...), branch_computations={%region_13.14_spmd, %region_14.15_spmd} | conditional | flops 1084489728 | bytes 38503096 | solution.py:229
  162.5 4.3 %fusion.11 = f32[8,1024,128]{2,1,0:T(8,128)} fusion(bf16[1024,1024]{1,0:T(8,128)(2,1)} %get-tuple-element.149, bf16[128,1024]{1,0:T(8,128)(2,1)S(1)} %get-tuple-element.150), kind=kOutput, calls=%fused_computation.9 | convolution fusion | flops 268435456 | bytes 6553600 | tf_op jit(solution)/shard_map/cond/branch_1_fun/rhe,khe->hrk/dot_general | solution.py:20
  166.8 4.1 %copy.88 = bf16[1024,1024]{0,1:T(8,128)(2,1)} copy(bf16[1024,1024]{1,0:T(8,128)(2,1)} %get-tuple-element.359) | data formatting | bytes 4194304 | tf_op jit(solution)/shard_map
  170.9 0.1 iota_compare_fusion
  171.0 6.4 %fusion.19 = f32[128,8,128]{2,0,1:T(8,128)S(1)} fusion(f32[8,1024,128]{2,1,0:T(8,128)} %fusion.11, bf16[1024,8,128]{0,2,1:T(8,128)(2,1)} %bitcast.152, f32[8,1024]{1,0:T(8,128)S(1)} %bitcast.174, f32[8,1024]{1,0:T(8,128)S(1)} %bitcast.176, pred[1024,128]{1,0:T(8,128)(4,1)S(1)} %iota_compare_fusion, bf16[1024,1024]{1,0:T(8,128)(2,1)S(1)} %copy-done.4, ...), kind=kOutput, calls=%fused_computation.17 | convolution fusion | flops 543162368 | bytes 9371648 | tf_op jit(solution)/shard_map/cond/branch_1_fun/hrk,rhe->khe/dot_general | solution.py:215
  177.4 0.2 copy.101
  177.6 3.8 %fusion.22 = bf16[8,128,128]{1,2,0:T(8,128)(2,1)S(1)} fusion(bf16[1024,8,128]{0,2,1:T(8,128)(2,1)} %bitcast.153, f32[8,1024,128]{2,1,0:T(8,128)} %fusion.11, f32[8,1024]{1,0:T(8,128)} %bitcast.175, pred[1024,128]{1,0:T(8,128)(4,1)S(1)} %iota_compare_fusion), kind=kOutput, calls=%fused_computation.18 | convolution fusion | flops 272760832 | bytes 6717440 | tf_op jit(solution)/shard_map/cond/branch_1_fun/hrk,rhe->khe/dot_general | solution.py:218
  181.4 0.9 copy.103
  182.3 0.9 copy.99
  (67 shorter events, 0.9 us)
Async XLA Ops:
  7.2 9.7 %copy-start.6 = (bf16[128,1024]{1,0:T(8,128)(2,1)S(1)}, bf16[128,1024]{1,0:T(8,128)(2,1)}, u32[]{:S(2)}) copy-start(bf16[128,1024]{1,0:T(8,128)(2,1)} %param.16) | copy-start | bytes 786436
  7.2 10.7 %copy-start.15 = (f32[128,7]{0,1:T(8,128)S(1)}, f32[128,7]{0,1:T(8,128)}, u32[]{:S(2)}) copy-start(f32[128,7]{0,1:T(8,128)} %param.21) | copy-start | bytes 10756
  7.2 34.1 %all-gather.7.cloned.1.call-start = ((), (), s32[]{:S(2)}) async-start(), calls=%async_computation.1 | async-start | bytes 2359296 | tf_op jit(solution)/shard_map/all_gather | solution.py:111
  9.1 62.8 %all-gather.5.cloned.1.call-start = ((), (), s32[]{:S(2)}) async-start(), calls=%async_computation | async-start | bytes 2359296 | tf_op jit(solution)/shard_map/all_gather | solution.py:112
  10.9 151.5 %all-gather.9.cloned.1.call-start = ((), (), s32[]{:S(2)}) async-start(), calls=%async_computation.2 | async-start | bytes 2359296 | tf_op jit(solution)/shard_map/all_gather | solution.py:199
  12.1 0.8 copy-start.3
  12.9 75.4 %collective-permute-start.1 = (f32[6,1024]{1,0:T(8,128)S(1)}, f32[6,1024]{1,0:T(8,128)S(1)}, u32[]{:S(2)}, u32[]{:S(2)}) collective-permute-start(f32[6,1024]{1,0:T(8,128)S(1)} %slice.119), channel_id=1, source_target_pairs={{4,0},{8,4},{12,8},{16,12},{20,16},{24,20},{28,24},{5,1},{9,5},{13... | collective-permute-start | bytes 73736 | tf_op jit(solution)/shard_map/ppermute | solution.py:16
  14.2 148.2 %all-gather.11.cloned.1.call-start = ((), (), s32[]{:S(2)}) async-start(), calls=%async_computation.3 | async-start | bytes 2359296 | tf_op jit(solution)/shard_map/all_gather | solution.py:200
  74.3 19.0 %copy-start = (f32[128,8,128]{0,2,1:T(8,128)}, f32[128,8,128]{0,2,1:T(8,128)S(1)}, u32[]{:S(2)}) copy-start(f32[128,8,128]{0,2,1:T(8,128)S(1)} %get-tuple-element.171) | copy-start | bytes 1572868
  74.4 13.9 %copy-start.10 = (f32[1024]{0:T(1024)S(1)}, f32[1024]{0:T(1024)}, u32[]{:S(2)}) copy-start(f32[1024]{0:T(1024)} %param.22) | copy-start | bytes 12292
  88.3 4.9 %copy-start.7 = (bf16[128,1024]{1,0:T(8,128)(2,1)S(1)}, bf16[128,1024]{1,0:T(8,128)(2,1)}, u32[]{:S(2)}) copy-start(bf16[128,1024]{1,0:T(8,128)(2,1)} %param.19) | copy-start | bytes 786436
  92.3 0.8 copy-start.1
  104.4 39.9 %collective-permute-start = (f32[6,1024]{1,0:T(8,128)}, f32[6,1024]{1,0:T(8,128)S(1)}, u32[]{:S(2)}, u32[]{:S(2)}) collective-permute-start(f32[6,1024]{1,0:T(8,128)} %slice.103), channel_id=1, source_target_pairs={{0,4},{4,8},{8,12},{12,16},{16,20},{20,24},{24,28},{1,5},{5,9},{9,... | collective-permute-start | bytes 73736 | tf_op jit(solution)/shard_map/ppermute | solution.py:16
  109.9 34.4 %copy-start.2 = (bf16[128,1024]{1,0:T(8,128)(2,1)S(1)}, bf16[128,1024]{1,0:T(8,128)(2,1)}, u32[]{:S(2)}) copy-start(bf16[128,1024]{1,0:T(8,128)(2,1)} %param.23) | copy-start | bytes 786436
  115.9 29.6 %copy-start.8 = (bf16[128,1024]{1,0:T(8,128)(2,1)S(1)}, bf16[128,1024]{1,0:T(8,128)(2,1)}, u32[]{:S(2)}) copy-start(bf16[128,1024]{1,0:T(8,128)(2,1)} %param.20) | copy-start | bytes 786436
  144.3 18.1 %copy-start.5 = (bf16[128,1024]{1,0:T(8,128)(2,1)S(1)}, bf16[128,1024]{1,0:T(8,128)(2,1)}, u32[]{:S(2)}) copy-start(bf16[128,1024]{1,0:T(8,128)(2,1)} %param.17) | copy-start | bytes 786436
  162.5 4.3 %copy-start.11 = (f32[1024,8]{0,1:T(8,128)}, f32[1024,8]{0,1:T(8,128)S(1)}, u32[]{:S(2)}) copy-start(f32[1024,8]{0,1:T(8,128)S(1)} %get-tuple-element.154) | copy-start | bytes 98308 | tf_op jit(solution)/shard_map/cond
  162.5 4.3 %copy-start.13 = (f32[1024,8]{0,1:T(8,128)}, f32[1024,8]{0,1:T(8,128)S(1)}, u32[]{:S(2)}) copy-start(f32[1024,8]{0,1:T(8,128)S(1)} %get-tuple-element.151) | copy-start | bytes 98308 | tf_op jit(solution)/shard_map/cond
  166.7 4.2 %copy-start.4 = (bf16[1024,1024]{1,0:T(8,128)(2,1)S(1)}, bf16[1024,1024]{1,0:T(8,128)(2,1)}, u32[]{:S(2)}) copy-start(bf16[1024,1024]{1,0:T(8,128)(2,1)} %get-tuple-element.149) | copy-start | bytes 6291460 | tf_op jit(solution)/shard_map/cond
  166.7 4.2 %copy-start.9 = (bf16[128,1024]{1,0:T(8,128)(2,1)S(1)}, bf16[128,1024]{1,0:T(8,128)(2,1)}, u32[]{:S(2)}) copy-start(bf16[128,1024]{1,0:T(8,128)(2,1)} %get-tuple-element.153) | copy-start | bytes 786436 | tf_op jit(solution)/shard_map/cond
  166.7 4.2 %copy-start.12 = (f32[1024,8]{0,1:T(8,128)S(1)}, f32[1024,8]{0,1:T(8,128)}, u32[]{:S(2)}) copy-start(f32[1024,8]{0,1:T(8,128)} %copy-done.11) | copy-start | bytes 98308 | tf_op jit(solution)/shard_map/cond
  166.8 4.2 %copy-start.14 = (f32[1024,8]{0,1:T(8,128)S(1)}, f32[1024,8]{0,1:T(8,128)}, u32[]{:S(2)}) copy-start(f32[1024,8]{0,1:T(8,128)} %copy-done.13) | copy-start | bytes 98308 | tf_op jit(solution)/shard_map/cond
Sparse Core Ops, SparseCore 0:
  10.4 30.8 all-gather.6
  43.8 28.0 all-gather.4
  73.8 27.7 all-gather.8
  109.2 30.4 all-gather.10
where the time goes:
time: 190 us
  blocking collectives  60.7 us (32%)
  waiting for transfers between devices  49.4 us (26%)
  matrix products  22.9 us (12%)
  local copies, waits for them, and re-layouts  22.2 us (12%)
  between operations  16.7 us (9%)
  other arithmetic  14.8 us (8%)
  starting transfers between devices  2.72 us (1%)
    all_gather x1, waiting for transfers between devices, shards(): lax.all_gather(value_rows, 'ctx', axis=0, tiled=True)  26.3 us
    all_gather x1, waiting for transfers between devices, shards(): lax.all_gather(key_rows, 'ctx', axis=0, tiled=True)  23 us
    all_gather x1, blocking collectives, shards(): lax.all_gather(delta_rows, 'ctx', axis=0, tiled=True)  17.9 us
    psum x1, blocking collectives, shards(): grad_filter, grad_gain = lax.psum((tap_terms, gain_terms), 'ctx')  14.2 us
    psum x1, blocking collectives, shards(): square_sum = lax.psum(jnp.sum(attn_wide * attn_wide, axis=1), 'chan')  11.7 us
    unnamed x27, local copies, waits for them, and re-layouts  10.6 us
    all_gather x1, blocking collectives, shards(): lax.all_gather(lse_rows, 'ctx', axis=0, tiled=True)  8.53 us
    psum x1, blocking collectives, shards(): row_dot = lax.psum(jnp.sum(scaled * attn_wide, axis=1), 'chan')  8.37 us
  transfers between devices with their start and end apart: 6, of which 2 were waited for; matrix products, arithmetic and copies ran while one was open for 19% of the time, Pallas kernels for 0%

commit v1 on v0

--- a/solution.py
+++ b/solution.py
@@ -131,7 +131,7 @@
     )
     lse_rows = lse_sets.T
     attn_wide = outputs.astype(jnp.float32)
-    square_sum = lax.psum(jnp.sum(attn_wide * attn_wide, axis=1), "chan")
+    square_sum = jnp.sum(lax.all_gather(jnp.sum(attn_wide * attn_wide, axis=1), "chan"), axis=0)
     inverse_rms = 1.0 / jnp.sqrt(square_sum / WIDTH + EPS)
     normed = attn_wide * inverse_rms[:, None] * norm_gain[None, :]
     gate_wide = gate_in.astype(jnp.float32)

time: 190 us -> 190 us (level)
    psum x1 -> x0, blocking collectives: 11.7 us -> none  [shards(): square_sum = lax.psum(jnp.sum(attn_wide * attn_wide, axis=1), 'chan')]
    all_gather x0 -> x1, blocking collectives: none -> 10.9 us  [shards(): lax.all_gather(jnp.sum(attn_wide * attn_wide, axis=1), 'chan')]
where the time goes in v1:
time: 190 us; the launch traced here: 189 us
  blocking collectives  59.9 us (32%)
  waiting for transfers between devices  49.4 us (26%)
  matrix products  22.9 us (12%)
  local copies, waits for them, and re-layouts  22.2 us (12%)
  between operations  16.7 us (9%)
  other arithmetic  14.9 us (8%)
  starting transfers between devices  2.72 us (1%)
    all_gather x1, waiting for transfers between devices, shards(): lax.all_gather(value_rows, 'ctx', axis=0, tiled=True)  26.3 us
    all_gather x1, waiting for transfers between devices, shards(): lax.all_gather(key_rows, 'ctx', axis=0, tiled=True)  23 us
    all_gather x1, blocking collectives, shards(): lax.all_gather(delta_rows, 'ctx', axis=0, tiled=True)  17.9 us
    psum x1, blocking collectives, shards(): grad_filter, grad_gain = lax.psum((tap_terms, gain_terms), 'ctx')  14.2 us
    all_gather x1, blocking collectives, shards(): lax.all_gather(jnp.sum(attn_wide * attn_wide, axis=1), 'chan')  10.9 us
    unnamed x27, local copies, waits for them, and re-layouts  10.6 us
    all_gather x1, blocking collectives, shards(): lax.all_gather(lse_rows, 'ctx', axis=0, tiled=True)  8.52 us
    psum x1, blocking collectives, shards(): row_dot = lax.psum(jnp.sum(scaled * attn_wide, axis=1), 'chan')  8.4 us
  transfers between devices with their start and end apart: 6, of which 2 were waited for; matrix products, arithmetic and copies ran while one was open for 19% of the time, Pallas kernels for 0%

profile of v1, /device:TPU:0, one launch (start us, length us, event | category | flops | bytes accessed | tf_op | source)
XLA Modules:
  0.0 188.9 jit_solution(10962953121709948678)
XLA Ops:
  7.2 1.8 copy.102
  9.1 1.8 copy.101
  11.0 1.1 convert_multiply_fusion.1
  12.1 0.8 copy-done.3
  12.9 1.3 collective-permute-start.1
  14.3 0.6 slice.80
  16.8 0.2 copy.103
  17.7 0.2 copy.107
  17.9 0.2 broadcast_in_dim.76
  18.1 0.2 reshape.215
  18.3 23.0 %all-gather.9.cloned.1.call-done = bf16[1024,1024]{0,1:T(8,128)(2,1)} async-done(((bf16[128,1024]{0,1:T(8,128)(2,1)}), bf16[1024,1024]{0,1:T(8,128)(2,1)}) %all-gather.9.cloned.1.call-update) | async-done | bytes 2097168 | tf_op jit(solution)/shard_map/all_gather | solution.py:111
  41.3 3.0 %copy.106 = bf16[1024,8,128]{2,0,1:T(8,128)(2,1)S(1)} copy(bf16[1024,8,128]{0,2,1:T(8,128)(2,1)} %bitcast.152) | data formatting | bytes 4194304
  44.4 1.2 while.35
  44.4 0.1 broadcast_compare_fusion.6
  44.6 0.5 fusion.130
  45.1 0.4 exponential_reduce_fusion.2
  45.6 26.3 %all-gather.7.cloned.1.call-done = bf16[1024,1024]{0,1:T(8,128)(2,1)} async-done(((bf16[128,1024]{0,1:T(8,128)(2,1)}), bf16[1024,1024]{0,1:T(8,128)(2,1)}) %all-gather.7.cloned.1.call-update) | async-done | bytes 2097168 | tf_op jit(solution)/shard_map/all_gather | solution.py:112
  71.9 2.4 %while.36 = (s32[]{:T(128)}, f32[128,8,128]{0,2,1:T(8,128)S(1)}, s32[]{:T(128)}, bf16[1024,8,128]{0,2,1:T(8,128)(2,1)}, bf16[1024,8,128]{2,0,1:T(8,128)(2,1)S(1)...) while((s32[]{:T(128)}, f32[128,8,128]{0,2,1:T(8,128)S(1)}, ...), condition=%wide.region_5.6_spmd.clone, body=%wide.region_4.5_spmd.clone.sunk | while | flops 270729856 | bytes 3549363 | solution.py:66
  72.0 0.1 broadcast_compare_fusion.7
  72.1 2.2 %fusion.134 = f32[128,8,128]{0,2,1:T(8,128)S(1)} fusion(f32[128,8,128]{0,2,1:T(8,128)S(1)} %get-tuple-element.697, bf16[128,8,128]{2,0,1:T(8,128)(2,1)S(1)} %get-tuple-element.713, f32[8,128]{1,0:T(8,128)S(1)} %get-tuple-element.714, bf16[1024,8,128]{2,0,1:T(8,128)(2,1)S(1)} %get-tuple-element.712, s32[]{:T(128)S(6)} %select_n.93, ...), kind=kOutput, calls=%fused_computation.44.clone.1 | convolution fusion | flops 270663680 | bytes 3478528 | tf_op jit(solution)/shard_map/while/body/hrk,khe->rhe/dot_general | solution.py:62
  74.4 1.0 multiply_reduce_fusion.10
  75.3 10.9 %all-gather.1 = f32[4,1,128]{2,1,0:T(1,128)S(1)} all-gather(f32[1,1,128]{2,1,0:T(1,128)S(1)} %bitcast.181), channel_id=2, replica_groups=mesh['ctx'=8,'chan'=4] {'chan'}, dimensions={0}, use_global_device_ids=true | all-gather | bytes 2560 | tf_op jit(solution)/shard_map/all_gather | solution.py:134
  86.2 1.2 copy.124
  87.5 4.0 %multiply_convert_fusion.1 = (bf16[128,1024]{1,0:T(8,128)(2,1)}, f32[128,1024]{1,0:T(8,128)S(1)}) fusion(f32[128,1024]{1,0:T(8,128)S(1)} %copy.124, f32[1024]{0:T(1024)S(1)} %copy-done.10, f32[128]{0:T(128)S(1)} %add_rsqrt_fusion, f32[6,1024]{1,0:T(8,128)S(1)} %collective-permute-done.1, f32[128,1024]{1,0:T(8,128)} %copy-done.3, f32[1024]{0:T(1024)S(1)} %bitcast.163, ...), kind=kLoop, calls=%fused_computation.133 | loop fusion | flops 3014656 | bytes 1892864 | tf_op jit(solution)/shard_map/convert_element_type | solution.py:166
  91.5 0.8 copy-done.1
  92.4 0.2 multiply_reduce_fusion
  92.6 8.4 %psum.21 = f32[128]{0:T(128)S(1)} all-reduce(f32[128]{0:T(128)S(1)} %get-tuple-element.413), channel_id=1, replica_groups=mesh['ctx'=8,'chan'=4] {'chan'}, use_global_device_ids=true, to_apply=%region_9.10 | all-reduce | flops 128 | bytes 1024 | tf_op jit(solution)/shard_map/psum | solution.py:171
  101.0 2.0 %subtract_convert_fusion = (bf16[128,1024]{1,0:T(8,128)(2,1)}, f32[128,1024]{1,0:T(8,128)S(1)}) fusion(f32[128,1024]{1,0:T(8,128)S(1)} %copy.124, f32[128]{0:T(128)S(1)} %fusion.102, f32[1024]{0:T(1024)S(1)} %copy-done.10, f32[128]{0:T(128)S(1)} %add_rsqrt_fusion, f32[128,1024]{1,0:T(8,128)} %copy-done.1, bf16[128,1024]{1,0:T(8,128)(2,1)} %param.19), kind=kLoop, calls=%fused_computation.137 | loop fusion | flops 1310720 | bytes 2102272 | tf_op jit(solution)/shard_map/convert_element_type | solution.py:174
  103.0 0.6 slice.103
  103.7 1.3 collective-permute-start
  104.9 1.0 copy.136
  105.9 0.2 copy.109
  106.2 1.1 multiply_reduce_fusion.8
  107.3 1.0 copy_bitcast_fusion
  108.3 0.9 broadcast.135
  109.2 5.9 %while.37 = (s32[]{:T(128)}, f32[128,8,128]{0,2,1:T(8,128)}, s32[]{:T(128)}, bf16[1024,8,128]{2,0,1:T(8,128)(2,1)S(1)}, bf16[128,8,128]{2,0,1:T(8,128)(2,1)S(1)}...) while((s32[]{:T(128)}, f32[128,8,128]{0,2,1:T(8,128)}, ...), condition=%wide.region_12.13_spmd.clone, body=%wide.region_11.12_spmd.clone.sunk | while | flops 405996160 | bytes 9058503 | solution.py:93
  109.2 1.7 fusion.140
  110.9 0.1 broadcast_compare_fusion.8
  111.1 4.1 %fusion.141 = f32[128,8,128]{0,2,1:T(8,128)} fusion(f32[128,8,128]{0,2,1:T(8,128)} %get-tuple-element.735, f32[8,512,128]{2,1,0:T(8,128)} %fusion.140, bf16[128,8,128]{2,0,1:T(8,128)(2,1)S(1)} %get-tuple-element.755, f32[8,128]{1,0:T(8,128)S(1)} %get-tuple-element.756, bf16[1024,8,128]{0,2,1:T(8,128)(2,1)} %get-tuple-element.754, s32[]{:T(128)S(6)} %select_n.95, ...), kind=kOutput, calls=%fused_computation.64.clone.1 | convolution fusion | flops 271712256 | bytes 5579776 | tf_op jit(solution)/shard_map/while/body/hrk,khe->rhe/dot_general | solution.py:89
  115.2 1.1 multiply_convert_fusion.3
  116.3 0.8 copy.125
  117.1 17.9 %all_gather.31 = f32[1024,8]{0,1:T(8,128)S(1)} all-gather(f32[128,8]{0,1:T(8,128)S(1)} %bitcast.179), channel_id=1, replica_groups=mesh['ctx'=8,'chan'=4] {'ctx'}, dimensions={0}, use_global_device_ids=true | all-gather | bytes 36864 | tf_op jit(solution)/shard_map/all_gather | solution.py:193
  135.0 8.5 %all_gather.29 = f32[1024,8]{0,1:T(8,128)S(1)} all-gather(f32[128,8]{0,1:T(8,128)S(1)} %bitcast.180), channel_id=1, replica_groups=mesh['ctx'=8,'chan'=4] {'ctx'}, dimensions={0}, use_global_device_ids=true | all-gather | bytes 36864 | tf_op jit(solution)/shard_map/all_gather | solution.py:192
  143.6 1.2 fusion.78
  144.8 1.2 multiply_reduce_fusion.1
  146.1 0.1 reshape.221
  146.2 0.1 reshape.222
  146.6 0.1 reduce_sum.185
  146.7 0.1 reduce_sum.187
  146.9 0.1 reduce_sum.189
  147.0 0.1 reduce_sum.191
  147.1 0.1 reduce_sum.193
  147.2 0.1 reduce_sum.195
  147.3 0.1 reduce_sum.197
  147.5 14.2 %all-reduce = (f32[128,7]{0,1:T(8,128)}, f32[1024]{0:T(1024)}) all-reduce(f32[128,7]{0,1:T(8,128)S(1)} %stack.31, f32[1024]{0:T(1024)S(1)} %get-tuple-element.412), channel_id=1, replica_groups=mesh['ctx'=8,'chan'=4] {'ctx'}, use_global_device_ids=true, to_apply=%region_29.30 | all-reduce | flops 1920 | bytes 15360 | tf_op jit(solution)/shard_map/psum | solution.py:169
  161.7 19.8 %conditional.1 = (f32[128,8,128]{0,2,1:T(8,128)S(1)}, bf16[128,1024]{1,0:T(8,128)(2,1)}) conditional(s32[]{:T(128)} %convert_element_type.91, () %tuple.33, (s32[128]{0:T(128)S(1)}, bf16[1024,1024]{1,0:T(8,128)(2,1)}, bf16[128,1024]{1,0:T(8,128)(2,1)S(1)}, f32[1024,8]{0,1:T(8,128)S(1)}, bf16[1024,1024]{1,0:T(8,128)(2,1)}, ...), branch_computations={%region_13.14_spmd, %region_14.15_spmd} | conditional | flops 1084489728 | bytes 38503096 | solution.py:229
  161.7 4.3 %fusion.11 = f32[8,1024,128]{2,1,0:T(8,128)} fusion(bf16[1024,1024]{1,0:T(8,128)(2,1)} %get-tuple-element.149, bf16[128,1024]{1,0:T(8,128)(2,1)S(1)} %get-tuple-element.150), kind=kOutput, calls=%fused_computation.9 | convolution fusion | flops 268435456 | bytes 6553600 | tf_op jit(solution)/shard_map/cond/branch_1_fun/rhe,khe->hrk/dot_general | solution.py:20
  166.0 4.1 %copy.115 = bf16[1024,1024]{0,1:T(8,128)(2,1)} copy(bf16[1024,1024]{1,0:T(8,128)(2,1)} %get-tuple-element.399) | data formatting | bytes 4194304 | tf_op jit(solution)/shard_map
  170.1 0.1 iota_compare_fusion
  170.2 6.4 %fusion.19 = f32[128,8,128]{2,0,1:T(8,128)S(1)} fusion(f32[8,1024,128]{2,1,0:T(8,128)} %fusion.11, bf16[1024,8,128]{0,2,1:T(8,128)(2,1)} %bitcast.153, f32[8,1024]{1,0:T(8,128)S(1)} %bitcast.175, f32[8,1024]{1,0:T(8,128)S(1)} %bitcast.177, pred[1024,128]{1,0:T(8,128)(4,1)S(1)} %iota_compare_fusion, bf16[1024,1024]{1,0:T(8,128)(2,1)S(1)} %copy-done.4, ...), kind=kOutput, calls=%fused_computation.17 | convolution fusion | flops 543162368 | bytes 9371648 | tf_op jit(solution)/shard_map/cond/branch_1_fun/hrk,rhe->khe/dot_general | solution.py:215
  176.6 0.2 copy.128
  176.9 3.8 %fusion.22 = bf16[8,128,128]{1,2,0:T(8,128)(2,1)S(1)} fusion(bf16[1024,8,128]{0,2,1:T(8,128)(2,1)} %bitcast.154, f32[8,1024,128]{2,1,0:T(8,128)} %fusion.11, f32[8,1024]{1,0:T(8,128)} %bitcast.176, pred[1024,128]{1,0:T(8,128)(4,1)S(1)} %iota_compare_fusion), kind=kOutput, calls=%fused_computation.18 | convolution fusion | flops 272760832 | bytes 6717440 | tf_op jit(solution)/shard_map/cond/branch_1_fun/hrk,rhe->khe/dot_general | solution.py:218
  180.6 0.8 copy.130
  181.6 0.8 copy.126
  (68 shorter events, 1.0 us)
Async XLA Ops:
  7.2 9.7 %copy-start.6 = (bf16[128,1024]{1,0:T(8,128)(2,1)S(1)}, bf16[128,1024]{1,0:T(8,128)(2,1)}, u32[]{:S(2)}) copy-start(bf16[128,1024]{1,0:T(8,128)(2,1)} %param.16) | copy-start | bytes 786436
  7.2 10.7 %copy-start.15 = (f32[128,7]{0,1:T(8,128)S(1)}, f32[128,7]{0,1:T(8,128)}, u32[]{:S(2)}) copy-start(f32[128,7]{0,1:T(8,128)} %param.21) | copy-start | bytes 10756
  7.2 34.1 %all-gather.9.cloned.1.call-start = ((), (), s32[]{:S(2)}) async-start(), calls=%async_computation.1 | async-start | bytes 2359296 | tf_op jit(solution)/shard_map/all_gather | solution.py:111
  9.1 62.8 %all-gather.7.cloned.1.call-start = ((), (), s32[]{:S(2)}) async-start(), calls=%async_computation | async-start | bytes 2359296 | tf_op jit(solution)/shard_map/all_gather | solution.py:112
  10.9 150.7 %all-gather.11.cloned.1.call-start = ((), (), s32[]{:S(2)}) async-start(), calls=%async_computation.2 | async-start | bytes 2359296 | tf_op jit(solution)/shard_map/all_gather | solution.py:199
  12.1 0.8 copy-start.3
  12.9 74.6 %collective-permute-start.1 = (f32[6,1024]{1,0:T(8,128)S(1)}, f32[6,1024]{1,0:T(8,128)S(1)}, u32[]{:S(2)}, u32[]{:S(2)}) collective-permute-start(f32[6,1024]{1,0:T(8,128)S(1)} %slice.119), channel_id=1, source_target_pairs={{4,0},{8,4},{12,8},{16,12},{20,16},{24,20},{28,24},{5,1},{9,5},{13... | collective-permute-start | bytes 73736 | tf_op jit(solution)/shard_map/ppermute | solution.py:16
  14.2 147.5 %all-gather.13.cloned.1.call-start = ((), (), s32[]{:S(2)}) async-start(), calls=%async_computation.3 | async-start | bytes 2359296 | tf_op jit(solution)/shard_map/all_gather | solution.py:200
  74.3 18.2 %copy-start = (f32[128,8,128]{0,2,1:T(8,128)}, f32[128,8,128]{0,2,1:T(8,128)S(1)}, u32[]{:S(2)}) copy-start(f32[128,8,128]{0,2,1:T(8,128)S(1)} %get-tuple-element.171) | copy-start | bytes 1572868
  74.4 13.2 %copy-start.10 = (f32[1024]{0:T(1024)S(1)}, f32[1024]{0:T(1024)}, u32[]{:S(2)}) copy-start(f32[1024]{0:T(1024)} %param.22) | copy-start | bytes 12292
  87.5 4.9 %copy-start.7 = (bf16[128,1024]{1,0:T(8,128)(2,1)S(1)}, bf16[128,1024]{1,0:T(8,128)(2,1)}, u32[]{:S(2)}) copy-start(bf16[128,1024]{1,0:T(8,128)(2,1)} %param.19) | copy-start | bytes 786436
  91.5 0.8 copy-start.1
  103.7 39.9 %collective-permute-start = (f32[6,1024]{1,0:T(8,128)}, f32[6,1024]{1,0:T(8,128)S(1)}, u32[]{:S(2)}, u32[]{:S(2)}) collective-permute-start(f32[6,1024]{1,0:T(8,128)} %slice.103), channel_id=1, source_target_pairs={{0,4},{4,8},{8,12},{12,16},{16,20},{20,24},{24,28},{1,5},{5,9},{9,... | collective-permute-start | bytes 73736 | tf_op jit(solution)/shard_map/ppermute | solution.py:16
  109.2 34.4 %copy-start.2 = (bf16[128,1024]{1,0:T(8,128)(2,1)S(1)}, bf16[128,1024]{1,0:T(8,128)(2,1)}, u32[]{:S(2)}) copy-start(bf16[128,1024]{1,0:T(8,128)(2,1)} %param.23) | copy-start | bytes 786436
  115.2 29.6 %copy-start.8 = (bf16[128,1024]{1,0:T(8,128)(2,1)S(1)}, bf16[128,1024]{1,0:T(8,128)(2,1)}, u32[]{:S(2)}) copy-start(bf16[128,1024]{1,0:T(8,128)(2,1)} %param.20) | copy-start | bytes 786436
  143.6 18.1 %copy-start.5 = (bf16[128,1024]{1,0:T(8,128)(2,1)S(1)}, bf16[128,1024]{1,0:T(8,128)(2,1)}, u32[]{:S(2)}) copy-start(bf16[128,1024]{1,0:T(8,128)(2,1)} %param.17) | copy-start | bytes 786436
  161.7 4.3 %copy-start.11 = (f32[1024,8]{0,1:T(8,128)}, f32[1024,8]{0,1:T(8,128)S(1)}, u32[]{:S(2)}) copy-start(f32[1024,8]{0,1:T(8,128)S(1)} %get-tuple-element.154) | copy-start | bytes 98308 | tf_op jit(solution)/shard_map/cond
  161.7 4.3 %copy-start.13 = (f32[1024,8]{0,1:T(8,128)}, f32[1024,8]{0,1:T(8,128)S(1)}, u32[]{:S(2)}) copy-start(f32[1024,8]{0,1:T(8,128)S(1)} %get-tuple-element.151) | copy-start | bytes 98308 | tf_op jit(solution)/shard_map/cond
  166.0 4.2 %copy-start.4 = (bf16[1024,1024]{1,0:T(8,128)(2,1)S(1)}, bf16[1024,1024]{1,0:T(8,128)(2,1)}, u32[]{:S(2)}) copy-start(bf16[1024,1024]{1,0:T(8,128)(2,1)} %get-tuple-element.149) | copy-start | bytes 6291460 | tf_op jit(solution)/shard_map/cond
  166.0 4.2 %copy-start.9 = (bf16[128,1024]{1,0:T(8,128)(2,1)S(1)}, bf16[128,1024]{1,0:T(8,128)(2,1)}, u32[]{:S(2)}) copy-start(bf16[128,1024]{1,0:T(8,128)(2,1)} %get-tuple-element.153) | copy-start | bytes 786436 | tf_op jit(solution)/shard_map/cond
  166.0 4.2 %copy-start.12 = (f32[1024,8]{0,1:T(8,128)S(1)}, f32[1024,8]{0,1:T(8,128)}, u32[]{:S(2)}) copy-start(f32[1024,8]{0,1:T(8,128)} %copy-done.11) | copy-start | bytes 98308 | tf_op jit(solution)/shard_map/cond
  166.0 4.2 %copy-start.14 = (f32[1024,8]{0,1:T(8,128)S(1)}, f32[1024,8]{0,1:T(8,128)}, u32[]{:S(2)}) copy-start(f32[1024,8]{0,1:T(8,128)} %copy-done.13) | copy-start | bytes 98308 | tf_op jit(solution)/shard_map/cond
Sparse Core Ops, SparseCore 0:
  10.4 30.8 all-gather.8
  43.8 28.0 all-gather.6
  73.8 27.7 all-gather.10
  108.4 30.4 all-gather.12
